TPU v7x, 128 devices: a whole 4x4x4 slice. The times are simulated.
128 devices in a mesh: gx: 16 (over x, y), gy: 8 (over z, core).
Axes of the slice: x: 4, y: 4, z: 4, core: 2. Of those that a mesh axis runs over, the one named last changes fastest.
Arguments:
- tensor: float32 [256, 512, 1024], P('gx', None, 'gy'), may hold values from -80 to 80
- start_basis: float32 [512, 384], replicated, may hold values from -6 to 6
Outputs:
- core: float32 [256, 384, 1024], P('gx', 'gy')
All inputs are finite; a program needn't handle non-finite values.
Results may differ from a plain program's by a relative error of at most 0.00019.
Values sent between devices are 32-bit elements; how exact they have to be, the bound alone decides.
A program may use at most 512 MiB of HBM per device.

v0:
```python
import jax
import jax.numpy as jnp
from jax import lax
from jax.sharding import PartitionSpec as P

ITERS = 2


def matmul(left, right):
    return jnp.dot(left, right, precision=lax.Precision.HIGHEST, preferred_element_type=jnp.float32)


def orthonormal(product):
    product_gram = matmul(product.T, product)
    lower = jnp.linalg.cholesky(product_gram)
    return jax.scipy.linalg.solve_triangular(lower, product.T, lower=True).T


def body(tensor, start_basis):
    local_gram = lax.dot_general(
        tensor,
        tensor,
        (((0, 2), (0, 2)), ((), ())),
        precision=lax.Precision.HIGHEST,
        preferred_element_type=jnp.float32,
    )
    gram = lax.psum(local_gram, ("gx", "gy"))
    basis = start_basis
    for sweep in range(ITERS):
        product = matmul(gram, basis)
        basis = orthonormal(product)
    core_local = jnp.einsum(
        "ar,kac->krc",
        basis,
        tensor,
        precision=lax.Precision.HIGHEST,
        preferred_element_type=jnp.float32,
    )
    return lax.all_to_all(core_local, "gy", split_axis=1, concat_axis=2, tiled=True)


def solution(mesh):
    placed = (P("gx", None, "gy"), P())
    return jax.shard_map(
        body, mesh=mesh, in_specs=placed, out_specs=P("gx", "gy", None), check_vma=False
    )
```

profile of v0, /device:TPU:1, one launch (start us, length us, event | category | flops | bytes accessed | tf_op | source)
XLA Modules:
  0.0 449.4 jit_solution(3196692239382905080)
XLA Ops:
  6.5 11.5 %convolution_bitcast_fusion.1 = f32[512,512]{1,0:T(8,128)} fusion(f32[16,512,128]{2,1,0:T(8,128)} %param.5), kind=kOutput, calls=%fused_computation.5 | convolution fusion | flops 6442450944 | bytes 5242880 | tf_op jit(solution)/shard_map/dot_general | solution.py:20
  18.1 150.7 %all-reduce.3.cloned.1.call-done = f32[512,512]{1,0:T(8,128)} async-done(((f32[512,512]{1,0:T(8,128)}), f32[512,512]{1,0:T(8,128)}) %all-reduce.3.cloned.1.call-update) | async-done | bytes 1048592 | tf_op jit(solution)/shard_map/psum | solution.py:27
  168.8 3.0 fusion.56
  171.8 1.4 fusion.57
  173.6 0.8 copy-done.2
  174.4 11.7 %cholesky.208 = f32[128,128]{1,0:T(8,128)S(1)} custom-call(f32[128,128]{1,0:T(8,128)S(1)} %cholesky.310), custom_call_target="Cholesky" | custom-call | tf_op jit(solution)/shard_map/jit(cholesky)/cholesky | solution.py:15
  186.1 9.8 %custom-call.20 = f32[1,128,128]{1,2,0:T(8,128)S(1)} custom-call(f32[1,128,128]{2,1,0:T(8,128)S(1)} %get-tuple-element.56), custom_call_target="InvertDiagBlocksLowerTriangular" | custom-call | tf_op jit(solution)/shard_map/jit(cholesky)/cholesky | solution.py:15
  196.0 1.2 constant_dynamic-update-slice_fusion.3
  197.3 1.2 convolution_subtract_fusion.5
  198.5 12.1 %cholesky.227 = f32[128,128]{1,0:T(8,128)S(1)} custom-call(f32[128,128]{1,0:T(8,128)S(1)} %cholesky.314), custom_call_target="Cholesky" | custom-call | tf_op jit(solution)/shard_map/jit(cholesky)/cholesky | solution.py:15
  210.6 9.8 %custom-call.21 = f32[1,128,128]{1,2,0:T(8,128)S(1)} custom-call(f32[1,128,128]{2,1,0:T(8,128)S(1)} %get-tuple-element.53), custom_call_target="InvertDiagBlocksLowerTriangular" | custom-call | tf_op jit(solution)/shard_map/jit(cholesky)/cholesky | solution.py:15
  220.6 1.1 convolution_subtract_fusion.7
  221.8 11.7 %cholesky.246 = f32[128,128]{1,0:T(8,128)S(1)} custom-call(f32[128,128]{1,0:T(8,128)S(1)} %convolution_subtract_fusion.7), custom_call_target="Cholesky" | custom-call | tf_op jit(solution)/shard_map/jit(cholesky)/cholesky | solution.py:15
  233.5 0.7 compare_reduce_fusion.3
  234.2 0.7 compare_reduce_fusion.4
  236.8 0.9 select_select_fusion.1
  237.7 8.7 %while.4 = (s32[]{:T(128)}, f32[384,384]{1,0:T(8,128)}, s32[3,2]{0,1:T(2,128)S(1)}, f32[3,128,128]{2,1,0:T(8,128)S(1)}, s32[]{:T(128)}) while((s32[]{:T(128)}, f32[384,384]{1,0:T(8,128)}, s32[3,2]{0,1:T(2,128)S(1)}, f32[3,128,128]{2,1,0:T(8,128)S(1)}, s32[]{:T(128)}) %tuple.47), condition=%wide.while_cond, body=%wide.while_body.sunk | while | flops 2 | bytes 131189 | solution.py:16
  238.3 2.3 bitcast_dynamic-update-slice_fusion.4
  241.3 2.3 bitcast_dynamic-update-slice_fusion.4
  244.2 2.2 bitcast_dynamic-update-slice_fusion.4
  246.4 29.7 %custom-call.22 = f32[3,128,128]{1,2,0:T(8,128)S(1)} custom-call(f32[3,128,128]{2,1,0:T(8,128)S(1)} %get-tuple-element.21), custom_call_target="InvertDiagBlocksLowerTriangular" | custom-call | tf_op jit(solution)/shard_map/jit(_solve_triangular)/triangular_solve | solution.py:16
  276.5 1.4 convolution_subtract_fusion.3
  278.4 1.9 convolution_subtract_fusion.2
  280.7 1.8 fusion
  282.6 1.4 fusion.58
  284.3 11.7 %cholesky.261 = f32[128,128]{1,0:T(8,128)S(1)} custom-call(f32[128,128]{1,0:T(8,128)S(1)} %cholesky.318), custom_call_target="Cholesky" | custom-call | tf_op jit(solution)/shard_map/jit(cholesky)/cholesky | solution.py:15
  296.1 0.6 compare_reduce_fusion.2
  296.7 10.0 %custom-call.23 = f32[1,128,128]{1,2,0:T(8,128)S(1)} custom-call(f32[1,128,128]{2,1,0:T(8,128)S(1)} %get-tuple-element.49), custom_call_target="InvertDiagBlocksLowerTriangular" | custom-call | tf_op jit(solution)/shard_map/jit(cholesky)/cholesky | solution.py:15
  307.3 11.7 %cholesky.280 = f32[128,128]{1,0:T(8,128)S(1)} custom-call(f32[128,128]{1,0:T(8,128)S(1)} %cholesky.322), custom_call_target="Cholesky" | custom-call | tf_op jit(solution)/shard_map/jit(cholesky)/cholesky | solution.py:15
  319.1 0.7 compare_reduce_fusion.1
  319.8 9.8 %custom-call.24 = f32[1,128,128]{1,2,0:T(8,128)S(1)} custom-call(f32[1,128,128]{2,1,0:T(8,128)S(1)} %get-tuple-element.46), custom_call_target="InvertDiagBlocksLowerTriangular" | custom-call | tf_op jit(solution)/shard_map/jit(cholesky)/cholesky | solution.py:15
  330.1 11.7 %cholesky.299 = f32[128,128]{1,0:T(8,128)S(1)} custom-call(f32[128,128]{1,0:T(8,128)S(1)} %convolution_subtract_fusion.6), custom_call_target="Cholesky" | custom-call | tf_op jit(solution)/shard_map/jit(cholesky)/cholesky | solution.py:15
  341.9 0.6 compare_reduce_fusion
  344.5 6.4 %while.5 = (s32[]{:T(128)}, f32[384,384]{1,0:T(8,128)S(1)}, s32[3,2]{0,1:T(2,128)S(1)}, f32[3,128,128]{2,1,0:T(8,128)S(1)}, s32[]{:T(128)}) while((s32[]{:T(128)}, f32[384,384]{1,0:T(8,128)S(1)}, s32[3,2]{0,1:T(2,128)S(1)}, f32[3,128,128]{2,1,0:T(8,128)S(1)}, s32[]{:T(128)}) %tuple.55), condition=%wide.while_cond.clone, body=%wide.while_body.clone.sunk | while | flops 2 | bytes 131189 | solution.py:16
  344.6 0.6 fusion.80
  345.2 1.4 bitcast_dynamic-update-slice_fusion.5
  346.7 0.6 fusion.80
  347.3 1.4 bitcast_dynamic-update-slice_fusion.5
  348.8 0.6 fusion.80
  349.4 1.4 bitcast_dynamic-update-slice_fusion.5
  350.8 29.7 %custom-call.25 = f32[3,128,128]{1,2,0:T(8,128)S(1)} custom-call(f32[3,128,128]{2,1,0:T(8,128)S(1)} %get-tuple-element.22), custom_call_target="InvertDiagBlocksLowerTriangular" | custom-call | tf_op jit(solution)/shard_map/jit(_solve_triangular)/triangular_solve | solution.py:16
  381.0 0.6 convolution_subtract_fusion.1
  382.0 1.0 convolution_subtract_fusion
  383.5 7.1 %convolution_bitcast_fusion = f32[16,384,128]{2,1,0:T(8,128)S(1)} fusion(f32[16,512,128]{2,1,0:T(8,128)} %param.5, f32[128,512]{1,0:T(8,128)S(1)} %fusion.30, f32[128,512]{1,0:T(8,128)S(1)} %fusion.32, f32[128,512]{1,0:T(8,128)S(1)} %fusion.18), kind=kOutput, calls=%fused_computation.4 | convolution fusion | flops 4832231424 | bytes 8126464 | tf_op jit(solution)/shard_map/ar,kac->krc/dot_general | solution.py:32
  390.6 1.8 copy.8
  392.4 41.7 %all_to_all.18 = f32[16,384,128]{2,0,1:T(8,128)S(1)} all-to-all(f32[16,384,128]{2,0,1:T(8,128)S(1)} %copy.8), channel_id=1, replica_groups=mesh['gx'=16,'gy'=8] {'gy'}, dimensions={1} | all-to-all | bytes 6291456 | tf_op jit(solution)/shard_map/all_to_all | solution.py:39
  434.1 3.5 copy.9
  437.6 4.5 %all_to_all.16 = f32[16,48,1024]{2,1,0:T(8,128)} reshape(f32[16,48,8,128]{3,2,1,0:T(8,128)} %copy.9) | data formatting | bytes 6291456 | tf_op jit(solution)/shard_map/all_to_all | solution.py:39
  (48 shorter events, 6.9 us)
Async XLA Ops:
  6.5 162.3 %copy-start = (f32[512,384]{1,0:T(8,128)S(1)}, f32[512,384]{1,0:T(8,128)}, u32[]{:S(2)}) copy-start(f32[512,384]{1,0:T(8,128)} %param.6) | copy-start | bytes 2359300
  6.5 162.3 %all-reduce.3.cloned.1.call-start = ((), (), s32[]{:S(2)}) async-start(), calls=%async_computation.1 | async-start | bytes 2097152 | tf_op jit(solution)/shard_map/psum | solution.py:27
  173.6 0.8 copy-start.2
  196.0 84.8 %copy-start.1 = (f32[512,512]{1,0:T(8,128)S(1)}, f32[512,512]{1,0:T(8,128)}, u32[]{:S(2)}) copy-start(f32[512,512]{1,0:T(8,128)} %all-reduce.3.cloned.1.call-done) | copy-start | bytes 3145732
Sparse Core Ops, SparseCore 0:
  18.2 150.5 all-reduce.2
where the time goes:
time: 453 us; the launch traced here: 449 us
  other arithmetic  174 us (38%)
  waiting for transfers between devices  151 us (33%)
  blocking collectives  41.7 us (9%)
  matrix products  38.5 us (8%)
  local copies, waits for them, and re-layouts  26.2 us (6%)
  between operations  18 us (4%)
    psum x1, waiting for transfers between devices, body(): gram = lax.psum(local_gram, ('gx', 'gy'))  151 us
    another operation x21, other arithmetic, orthonormal(): lower = jnp.linalg.cholesky(product_gram)  114 us
    another operation x5, other arithmetic, orthonormal(): return jax.scipy.linalg.solve_triangular(lower, product.T, lower=True).T  60.3 us
    all_to_all x1, blocking collectives, body(): lax.all_to_all(core_local, 'gy', split_axis=1, concat_axis=2, tiled=True)  41.7 us
    another operation x21, local copies, waits for them, and re-layouts, orthonormal(): return jax.scipy.linalg.solve_triangular(lower, product.T, lower=True).T  15 us
    dot_general x1, matrix products, body(): lax.dot_general(tensor, tensor, (((0, 2), (0, 2)), ((), ())), precision=l...  11.5 us
  transfers between devices with their start and end apart: 1, of which 1 were waited for; matrix products, arithmetic and copies ran while one was open for 0% of the time, Pallas kernels for 0%

commit v1 on v0

--- a/solution.py
+++ b/solution.py
@@ -2,6 +2,7 @@
 import jax.numpy as jnp
 from jax import lax
 from jax.sharding import PartitionSpec as P
+from jax.lax import psum
 
 ITERS = 2
 
@@ -24,7 +25,7 @@
         precision=lax.Precision.HIGHEST,
         preferred_element_type=jnp.float32,
     )
-    gram = lax.psum(local_gram, ("gx", "gy"))
+    gram = psum(psum(local_gram, "gy"), "gx")
     basis = start_basis
     for sweep in range(ITERS):
         product = matmul(gram, basis)

time: 453 us -> 462 us (1.020)
    psum x1 -> x2, waiting for transfers between devices: 151 us -> 154 us  [body(): gram = psum(psum(local_gram, 'gy'), 'gx')]
  transfers between devices with their start and end apart: 1 -> 2, of which waited for: 1 -> 2; matrix products, arithmetic and copies ran while one was open for 0% -> 0% of each run, Pallas kernels for 0% -> 0%
where the time goes in v1:
time: 462 us; the launch traced here: 458 us
  other arithmetic  174 us (38%)
  waiting for transfers between devices  154 us (33%)
  blocking collectives  44.3 us (10%)
  matrix products  40.9 us (9%)
  local copies, waits for them, and re-layouts  27.1 us (6%)
  between operations  18 us (4%)
    psum x2, waiting for transfers between devices, body(): gram = psum(psum(local_gram, 'gy'), 'gx')  154 us
    another operation x21, other arithmetic, orthonormal(): lower = jnp.linalg.cholesky(product_gram)  114 us
    another operation x5, other arithmetic, orthonormal(): return jax.scipy.linalg.solve_triangular(lower, product.T, lower=True).T  60.3 us
    all_to_all x1, blocking collectives, body(): lax.all_to_all(core_local, 'gy', split_axis=1, concat_axis=2, tiled=True)  44.3 us
    another operation x21, local copies, waits for them, and re-layouts, orthonormal(): return jax.scipy.linalg.solve_triangular(lower, product.T, lower=True).T  15 us
    dot_general x1, matrix products, body(): lax.dot_general(tensor, tensor, (((0, 2), (0, 2)), ((), ())), precision=l...  11.3 us
  transfers between devices with their start and end apart: 2, of which 2 were waited for; matrix products, arithmetic and copies ran while one was open for 0% of the time, Pallas kernels for 0%

profile of v1, /device:TPU:1, one launch (start us, length us, event | category | flops | bytes accessed | tf_op | source)
XLA Modules:
  0.0 458.4 jit_solution(1013227493495849569)
XLA Ops:
  6.5 11.3 %convolution_bitcast_fusion.1 = f32[512,512]{1,0:T(8,128)} fusion(f32[16,512,128]{2,1,0:T(8,128)} %param.5), kind=kOutput, calls=%fused_computation.5 | convolution fusion | flops 6442450944 | bytes 5242880 | tf_op jit(solution)/shard_map/dot_general | solution.py:21
  18.1 63.8 %all-reduce.4.cloned.1.call-done = f32[512,512]{1,0:T(8,128)} async-done(((f32[512,512]{1,0:T(8,128)}), f32[512,512]{1,0:T(8,128)}) %all-reduce.4.cloned.1.call-update) | async-done | bytes 1048592 | tf_op jit(solution)/shard_map/psum | solution.py:28
  81.9 89.8 %all-reduce.6.cloned.1.call-done = f32[512,512]{1,0:T(8,128)} async-done(((f32[512,512]{1,0:T(8,128)}), f32[512,512]{1,0:T(8,128)}) %all-reduce.6.cloned.1.call-update) | async-done | bytes 1048592 | tf_op jit(solution)/shard_map/psum | solution.py:28
  171.7 3.0 fusion.56
  174.8 1.4 fusion.57
  176.5 0.8 copy-done.3
  177.3 11.7 %cholesky.208 = f32[128,128]{1,0:T(8,128)S(1)} custom-call(f32[128,128]{1,0:T(8,128)S(1)} %cholesky.310), custom_call_target="Cholesky" | custom-call | tf_op jit(solution)/shard_map/jit(cholesky)/cholesky | solution.py:16
  189.1 9.8 %custom-call.20 = f32[1,128,128]{1,2,0:T(8,128)S(1)} custom-call(f32[1,128,128]{2,1,0:T(8,128)S(1)} %get-tuple-element.56), custom_call_target="InvertDiagBlocksLowerTriangular" | custom-call | tf_op jit(solution)/shard_map/jit(cholesky)/cholesky | solution.py:16
  199.0 1.2 constant_dynamic-update-slice_fusion.3
  200.2 1.2 convolution_subtract_fusion.5
  201.4 12.1 %cholesky.227 = f32[128,128]{1,0:T(8,128)S(1)} custom-call(f32[128,128]{1,0:T(8,128)S(1)} %cholesky.314), custom_call_target="Cholesky" | custom-call | tf_op jit(solution)/shard_map/jit(cholesky)/cholesky | solution.py:16
  213.5 9.8 %custom-call.21 = f32[1,128,128]{1,2,0:T(8,128)S(1)} custom-call(f32[1,128,128]{2,1,0:T(8,128)S(1)} %get-tuple-element.53), custom_call_target="InvertDiagBlocksLowerTriangular" | custom-call | tf_op jit(solution)/shard_map/jit(cholesky)/cholesky | solution.py:16
  223.6 1.1 convolution_subtract_fusion.7
  224.7 11.7 %cholesky.246 = f32[128,128]{1,0:T(8,128)S(1)} custom-call(f32[128,128]{1,0:T(8,128)S(1)} %convolution_subtract_fusion.7), custom_call_target="Cholesky" | custom-call | tf_op jit(solution)/shard_map/jit(cholesky)/cholesky | solution.py:16
  236.4 0.7 compare_reduce_fusion.3
  237.2 0.6 compare_reduce_fusion.4
  239.7 0.9 select_select_fusion.1
  240.6 8.8 %while.4 = (s32[]{:T(128)}, f32[384,384]{1,0:T(8,128)}, s32[3,2]{0,1:T(2,128)S(1)}, f32[3,128,128]{2,1,0:T(8,128)S(1)}, s32[]{:T(128)}) while((s32[]{:T(128)}, f32[384,384]{1,0:T(8,128)}, s32[3,2]{0,1:T(2,128)S(1)}, f32[3,128,128]{2,1,0:T(8,128)S(1)}, s32[]{:T(128)}) %tuple.47), condition=%wide.while_cond, body=%wide.while_body.sunk | while | flops 2 | bytes 131189 | solution.py:17
  241.3 2.3 bitcast_dynamic-update-slice_fusion.4
  244.2 2.3 bitcast_dynamic-update-slice_fusion.4
  247.2 2.2 bitcast_dynamic-update-slice_fusion.4
  249.4 29.7 %custom-call.22 = f32[3,128,128]{1,2,0:T(8,128)S(1)} custom-call(f32[3,128,128]{2,1,0:T(8,128)S(1)} %get-tuple-element.21), custom_call_target="InvertDiagBlocksLowerTriangular" | custom-call | tf_op jit(solution)/shard_map/jit(_solve_triangular)/triangular_solve | solution.py:17
  279.5 1.4 convolution_subtract_fusion.3
  281.3 1.9 convolution_subtract_fusion.2
  283.7 1.8 fusion
  285.5 1.4 fusion.58
  287.2 0.8 copy-done.2
  288.1 11.7 %cholesky.261 = f32[128,128]{1,0:T(8,128)S(1)} custom-call(f32[128,128]{1,0:T(8,128)S(1)} %cholesky.318), custom_call_target="Cholesky" | custom-call | tf_op jit(solution)/shard_map/jit(cholesky)/cholesky | solution.py:16
  299.8 0.7 compare_reduce_fusion.2
  300.5 10.0 %custom-call.23 = f32[1,128,128]{1,2,0:T(8,128)S(1)} custom-call(f32[1,128,128]{2,1,0:T(8,128)S(1)} %get-tuple-element.49), custom_call_target="InvertDiagBlocksLowerTriangular" | custom-call | tf_op jit(solution)/shard_map/jit(cholesky)/cholesky | solution.py:16
  310.6 1.2 constant_dynamic-update-slice_fusion.1
  311.7 1.2 convolution_subtract_fusion.4
  312.9 11.7 %cholesky.280 = f32[128,128]{1,0:T(8,128)S(1)} custom-call(f32[128,128]{1,0:T(8,128)S(1)} %cholesky.322), custom_call_target="Cholesky" | custom-call | tf_op jit(solution)/shard_map/jit(cholesky)/cholesky | solution.py:16
  325.3 9.8 %custom-call.24 = f32[1,128,128]{1,2,0:T(8,128)S(1)} custom-call(f32[1,128,128]{2,1,0:T(8,128)S(1)} %get-tuple-element.46), custom_call_target="InvertDiagBlocksLowerTriangular" | custom-call | tf_op jit(solution)/shard_map/jit(cholesky)/cholesky | solution.py:16
  335.3 1.1 convolution_subtract_fusion.6
  336.5 11.7 %cholesky.299 = f32[128,128]{1,0:T(8,128)S(1)} custom-call(f32[128,128]{1,0:T(8,128)S(1)} %convolution_subtract_fusion.6), custom_call_target="Cholesky" | custom-call | tf_op jit(solution)/shard_map/jit(cholesky)/cholesky | solution.py:16
  348.2 0.6 compare_reduce_fusion
  350.8 6.4 %while.5 = (s32[]{:T(128)}, f32[384,384]{1,0:T(8,128)S(1)}, s32[3,2]{0,1:T(2,128)S(1)}, f32[3,128,128]{2,1,0:T(8,128)S(1)}, s32[]{:T(128)}) while((s32[]{:T(128)}, f32[384,384]{1,0:T(8,128)S(1)}, s32[3,2]{0,1:T(2,128)S(1)}, f32[3,128,128]{2,1,0:T(8,128)S(1)}, s32[]{:T(128)}) %tuple.57), condition=%wide.while_cond.clone, body=%wide.while_body.clone.sunk | while | flops 2 | bytes 131189 | solution.py:17
  351.5 1.4 bitcast_dynamic-update-slice_fusion.5
  353.6 1.4 bitcast_dynamic-update-slice_fusion.5
  355.8 1.4 bitcast_dynamic-update-slice_fusion.5
  357.2 29.7 %custom-call.25 = f32[3,128,128]{1,2,0:T(8,128)S(1)} custom-call(f32[3,128,128]{2,1,0:T(8,128)S(1)} %get-tuple-element.22), custom_call_target="InvertDiagBlocksLowerTriangular" | custom-call | tf_op jit(solution)/shard_map/jit(_solve_triangular)/triangular_solve | solution.py:17
  388.4 1.0 convolution_subtract_fusion
  389.8 7.1 %convolution_bitcast_fusion = f32[16,384,128]{2,1,0:T(8,128)S(1)} fusion(f32[16,512,128]{2,1,0:T(8,128)} %param.5, f32[128,512]{1,0:T(8,128)S(1)} %fusion.30, f32[128,512]{1,0:T(8,128)S(1)} %fusion.32, f32[128,512]{1,0:T(8,128)S(1)} %fusion.18), kind=kOutput, calls=%fused_computation.4 | convolution fusion | flops 4832231424 | bytes 8126464 | tf_op jit(solution)/shard_map/ar,kac->krc/dot_general | solution.py:33
  396.9 1.8 copy.8
  398.8 44.3 %all_to_all.18 = f32[16,384,128]{2,0,1:T(8,128)S(1)} all-to-all(f32[16,384,128]{2,0,1:T(8,128)S(1)} %copy.8), channel_id=1, replica_groups=mesh['gx'=16,'gy'=8] {'gy'}, dimensions={1} | all-to-all | bytes 6291456 | tf_op jit(solution)/shard_map/all_to_all | solution.py:40
  443.1 3.5 copy.9
  446.5 4.5 all_to_all.16
  (53 shorter events, 9.4 us)
Async XLA Ops:
  6.5 165.2 %copy-start = (f32[512,384]{1,0:T(8,128)S(1)}, f32[512,384]{1,0:T(8,128)}, u32[]{:S(2)}) copy-start(f32[512,384]{1,0:T(8,128)} %param.6) | copy-start | bytes 2359300
  6.5 75.4 %all-reduce.4.cloned.1.call-start = ((), (), s32[]{:S(2)}) async-start(), calls=%async_computation.1 | async-start | bytes 2097152 | tf_op jit(solution)/shard_map/psum | solution.py:28
  17.9 153.9 %all-reduce.6.cloned.1.call-start = ((), (), s32[]{:S(2)}) async-start(), calls=%async_computation.2 | async-start | bytes 2097152 | tf_op jit(solution)/shard_map/psum | solution.py:28
  176.5 0.8 copy-start.3
  198.9 84.7 %copy-start.1 = (f32[512,512]{1,0:T(8,128)S(1)}, f32[512,512]{1,0:T(8,128)}, u32[]{:S(2)}) copy-start(f32[512,512]{1,0:T(8,128)} %all-reduce.6.cloned.1.call-done) | copy-start | bytes 3145732
  287.2 0.8 copy-start.2
Sparse Core Ops, SparseCore 0:
  18.0 63.8 all-reduce.3
  85.1 86.5 all-reduce.5
